TPU v7x, 32 devices: a whole 2x2x4 slice. The times are simulated.
32 devices in a mesh: blk: 8 (over z, x), head: 4 (over y, core).
Axes of the slice: x: 2, y: 2, z: 4, core: 2. Of those that a mesh axis runs over, the one named last changes fastest.
Arguments:
- inputs: bfloat16 [16384, 768], P(('blk', 'head')), may hold values from -6 to 6
- segments: int32 [16384], replicated, may hold values from 0 to 15, never falling along the last dimension, each value on 1 to 2048 neighbouring positions
- cotangent: bfloat16 [16384, 768], P(('blk', 'head')), may hold values from -6 to 6
- w_qkv: bfloat16 [768, 2304], P(('blk', 'head')), may hold values from -0.3125 to 0.3125
- q_bias: bfloat16 [768], P(('blk', 'head')), may hold values from -3 to 3
- v_bias: bfloat16 [768], P(('blk', 'head')), may hold values from -3 to 3
- w_out: bfloat16 [768, 768], P(('blk', 'head')), may hold values from -1.25 to 1.25
- out_bias: bfloat16 [768], P(('blk', 'head')), may hold values from -3 to 3
- ln1_gain: bfloat16 [768], P(('blk', 'head')), may hold values from 0.5 to 1.5
- ln1_bias: bfloat16 [768], P(('blk', 'head')), may hold values from -2 to 2
- w_in: bfloat16 [768, 3072], P(('blk', 'head')), may hold values from -0.21875 to 0.21875
- in_bias: bfloat16 [3072], P(('blk', 'head')), may hold values from -3 to 3
- w_down: bfloat16 [3072, 768], P(('blk', 'head')), may hold values from -0.15625 to 0.15625
- down_bias: bfloat16 [768], P(('blk', 'head')), may hold values from -3 to 3
- ln2_gain: bfloat16 [768], P(('blk', 'head')), may hold values from 0.5 to 1.5
- ln2_bias: bfloat16 [768], P(('blk', 'head')), may hold values from -2 to 2
Outputs:
- outputs: bfloat16 [16384, 768], P(('blk', 'head'))
- d_inputs: bfloat16 [16384, 768], P(('blk', 'head'))
- d_w_qkv: float32 [768, 2304], P(('blk', 'head'))
- d_q_bias: float32 [768], P(('blk', 'head'))
- d_v_bias: float32 [768], P(('blk', 'head'))
- d_w_out: float32 [768, 768], P(('blk', 'head'))
- d_out_bias: float32 [768], P(('blk', 'head'))
- d_ln1_gain: float32 [768], P(('blk', 'head'))
- d_ln1_bias: float32 [768], P(('blk', 'head'))
- d_w_in: float32 [768, 3072], P(('blk', 'head'))
- d_in_bias: float32 [3072], P(('blk', 'head'))
- d_w_down: float32 [3072, 768], P(('blk', 'head'))
- d_down_bias: float32 [768], P(('blk', 'head'))
- d_ln2_gain: float32 [768], P(('blk', 'head'))
- d_ln2_bias: float32 [768], P(('blk', 'head'))
Inputs may be any that keep to these rules, and one draw needn't show every extreme that they name: `segments`: segment numbers never fall along the tokens; every number from 0 to 15 has 1 to 2048 tokens, and some number has exactly 2048.
All inputs are finite; a program needn't handle non-finite values.
Results may differ from a plain program's by a relative error of at most 0.017.
The roundings to bfloat16 on the way count: a program that leaves them out, or rounds other values in their place, can miss the bound.
Values may be sent and summed in bfloat16 or wider, within the bound.
A program may use at most 128 MiB of HBM per device.

v0:
```python
import jax
import jax.numpy as jnp
from jax import lax
from jax.sharding import PartitionSpec as P

HEAD_DIM = 64


def padded(block, sides, width):
    for axis, dim in sides:
        count = lax.axis_size(axis)
        forward = [(i, i + 1) for i in range(count - 1)]
        backward = [(target, source) for source, target in forward]
        low = lax.ppermute(
            lax.slice_in_dim(block, block.shape[dim] - width, None, axis=dim), axis, forward
        )
        high = lax.ppermute(lax.slice_in_dim(block, 0, width, axis=dim), axis, backward)
        block = jnp.concatenate([low, block, high], axis=dim)
    return block


def from_behind(value, axis, steps):
    count = lax.axis_size(axis)
    first, last = (max(0, -steps), min(count, count - steps))
    return lax.ppermute(value, axis, [(source, source + steps) for source in range(first, last)])


def layer_norm(values, gain, shift_vec):
    centre = jnp.mean(values, axis=-1, keepdims=True)
    centered = values - centre
    spread = jnp.mean(centered * centered, axis=-1, keepdims=True)
    return centered * lax.rsqrt(spread + 1e-05) * gain + shift_vec


def gelu_exact(values):
    return jax.nn.gelu(values, approximate=False)


def doc_scores(q_tile, k_tile, q_label, k_label, score_scale):
    raw_scores = (
        jnp.einsum("qhd,khd->hqk", q_tile, k_tile, preferred_element_type=jnp.float32) * score_scale
    )
    same_doc = (q_label[:, None] == k_label[None, :])[None]
    return (raw_scores, same_doc)


def sweep(step_fn, carry, q_first, tile_rows, key_count, key_rows, value_rows, window_labels):

    def one_key(key_index, state):
        k_first = q_first + key_index * tile_rows
        k_tile = lax.dynamic_slice_in_dim(key_rows, k_first, tile_rows, 0)
        v_tile = lax.dynamic_slice_in_dim(value_rows, k_first, tile_rows, 0)
        k_label = lax.dynamic_slice_in_dim(window_labels, k_first, tile_rows, 0)
        return step_fn(state, k_first, k_tile, v_tile, k_label)

    return lax.fori_loop(0, key_count, one_key, carry)


def attend_forward(queries, key_rows, value_rows, q_labels, window_labels):
    total_rows, groups, head_dim = queries.shape
    tile_rows = min(512, total_rows)
    query_count = total_rows // tile_rows
    key_count = 2 * query_count + 1
    score_scale = head_dim ** (-0.5)

    def one_query(q_index, results):
        attended, log_sums = results
        q_first = q_index * tile_rows
        q_tile = lax.dynamic_slice_in_dim(queries, q_first, tile_rows, 0)
        q_label = lax.dynamic_slice_in_dim(q_labels, q_first, tile_rows, 0)

        def stats(state, k_first, k_tile, v_tile, k_label):
            top_score, denominator = state
            raw_scores, same_doc = doc_scores(q_tile, k_tile, q_label, k_label, score_scale)
            masked = jnp.where(same_doc, raw_scores, -1e30)
            new_top = jnp.maximum(top_score, jnp.max(masked, axis=-1))
            weights_e = jnp.where(same_doc, jnp.exp(raw_scores - new_top[:, :, None]), 0.0)
            return (
                new_top,
                denominator * jnp.exp(top_score - new_top) + jnp.sum(weights_e, axis=-1),
            )

        start_state = (
            jnp.full((groups, tile_rows), -1e30, jnp.float32),
            jnp.zeros((groups, tile_rows), jnp.float32),
        )
        top_score, denominator = sweep(
            stats, start_state, q_first, tile_rows, key_count, key_rows, value_rows, window_labels
        )
        log_sum = top_score + jnp.log(denominator)

        def add_values(running, k_first, k_tile, v_tile, k_label):
            raw_scores, same_doc = doc_scores(q_tile, k_tile, q_label, k_label, score_scale)
            softmax_w = jnp.where(same_doc, jnp.exp(raw_scores - log_sum[:, :, None]), 0.0).astype(
                jnp.bfloat16
            )
            return running + jnp.einsum(
                "hqk,khd->qhd", softmax_w, v_tile, preferred_element_type=jnp.float32
            )

        tile_out = sweep(
            add_values,
            jnp.zeros((tile_rows, groups, head_dim), jnp.float32),
            q_first,
            tile_rows,
            key_count,
            key_rows,
            value_rows,
            window_labels,
        )
        attended = lax.dynamic_update_slice_in_dim(attended, tile_out, q_first, 0)
        log_sums = lax.dynamic_update_slice_in_dim(log_sums, log_sum, q_first, 1)
        return (attended, log_sums)

    start_results = (
        jnp.zeros((total_rows, groups, head_dim), jnp.float32),
        jnp.zeros((groups, total_rows), jnp.float32),
    )
    return lax.fori_loop(0, query_count, one_query, start_results)


def attend_backward(
    queries, key_rows, value_rows, q_labels, window_labels, attended, log_sums, d_attended
):
    total_rows, groups, head_dim = queries.shape
    tile_rows = min(512, total_rows)
    query_count = total_rows // tile_rows
    key_count = 2 * query_count + 1
    score_scale = head_dim ** (-0.5)

    def one_query(q_index, state):
        d_queries, d_window = state
        q_first = q_index * tile_rows
        q_tile = lax.dynamic_slice_in_dim(queries, q_first, tile_rows, 0)
        q_label = lax.dynamic_slice_in_dim(q_labels, q_first, tile_rows, 0)
        o_tile = lax.dynamic_slice_in_dim(attended, q_first, tile_rows, 0)
        do_tile = lax.dynamic_slice_in_dim(d_attended, q_first, tile_rows, 0)
        log_sum = lax.dynamic_slice_in_dim(log_sums, q_first, tile_rows, 1)
        delta_row = jnp.sum(do_tile.astype(jnp.float32) * o_tile, axis=-1).T

        def grads_step(inner, k_first, k_tile, v_tile, k_label):
            dq_tile, window_grads = inner
            raw_scores, same_doc = doc_scores(q_tile, k_tile, q_label, k_label, score_scale)
            softmax_w = jnp.where(same_doc, jnp.exp(raw_scores - log_sum[:, :, None]), 0.0)
            d_weights = jnp.einsum(
                "qhd,khd->hqk", do_tile, v_tile, preferred_element_type=jnp.float32
            )
            d_scores = (softmax_w * (d_weights - delta_row[:, :, None])).astype(jnp.bfloat16)
            dq_tile = (
                dq_tile
                + jnp.einsum("hqk,khd->qhd", d_scores, k_tile, preferred_element_type=jnp.float32)
                * score_scale
            )
            dk_part = (
                jnp.einsum("hqk,qhd->khd", d_scores, q_tile, preferred_element_type=jnp.float32)
                * score_scale
            )
            dv_part = jnp.einsum(
                "hqk,qhd->khd",
                softmax_w.astype(jnp.bfloat16),
                do_tile,
                preferred_element_type=jnp.float32,
            )
            key_value_part = jnp.stack([dk_part, dv_part], axis=1)
            current = lax.dynamic_slice_in_dim(window_grads, k_first, tile_rows, 0)
            window_grads = lax.dynamic_update_slice_in_dim(
                window_grads, current + key_value_part, k_first, 0
            )
            return (dq_tile, window_grads)

        start_inner = (jnp.zeros((tile_rows, groups, head_dim), jnp.float32), d_window)
        dq_tile, d_window = sweep(
            grads_step,
            start_inner,
            q_first,
            tile_rows,
            key_count,
            key_rows,
            value_rows,
            window_labels,
        )
        d_queries = lax.dynamic_update_slice_in_dim(d_queries, dq_tile, q_first, 0)
        return (d_queries, d_window)

    start_state = (
        jnp.zeros((total_rows, groups, head_dim), jnp.float32),
        jnp.zeros((3 * total_rows, 2, groups, head_dim), jnp.float32),
    )
    return lax.fori_loop(0, query_count, one_query, start_state)


def body(
    inputs,
    segments,
    cotangent,
    w_qkv,
    q_bias,
    v_bias,
    w_out,
    out_bias,
    ln1_gain,
    ln1_bias,
    w_in,
    in_bias,
    w_down,
    down_bias,
    ln2_gain,
    ln2_bias,
):
    gathered = (
        lax.all_gather(w_qkv, ("blk", "head"), axis=0, tiled=True),
        lax.all_gather(q_bias, ("blk", "head"), axis=0, tiled=True),
        lax.all_gather(v_bias, ("blk", "head"), axis=0, tiled=True),
        lax.all_gather(w_out, ("blk", "head"), axis=0, tiled=True),
        lax.all_gather(out_bias, ("blk", "head"), axis=0, tiled=True),
        lax.all_gather(ln1_gain, ("blk", "head"), axis=0, tiled=True),
        lax.all_gather(ln1_bias, ("blk", "head"), axis=0, tiled=True),
        lax.all_gather(w_in, ("blk", "head"), axis=0, tiled=True),
        lax.all_gather(in_bias, ("blk", "head"), axis=0, tiled=True),
        lax.all_gather(w_down, ("blk", "head"), axis=0, tiled=True),
        lax.all_gather(down_bias, ("blk", "head"), axis=0, tiled=True),
        lax.all_gather(ln2_gain, ("blk", "head"), axis=0, tiled=True),
        lax.all_gather(ln2_bias, ("blk", "head"), axis=0, tiled=True),
    )
    (
        g_qkv,
        g_q_bias,
        g_v_bias,
        g_out,
        g_out_bias,
        g_ln1_gain,
        g_ln1_bias,
        g_in,
        g_in_bias,
        g_down,
        g_down_bias,
        g_ln2_gain,
        g_ln2_bias,
    ) = gathered
    tok_rows, model_width = inputs.shape
    qkv_bias = jnp.concatenate(
        [
            g_q_bias.astype(jnp.float32),
            jnp.zeros((model_width,), jnp.float32),
            g_v_bias.astype(jnp.float32),
        ]
    )
    mixed_qkv = (
        (jnp.dot(inputs, g_qkv, preferred_element_type=jnp.float32) + qkv_bias)
        .astype(jnp.bfloat16)
        .reshape(tok_rows, 3, model_width)
    )
    head_rows = lax.all_to_all(mixed_qkv, "head", split_axis=2, concat_axis=0, tiled=True)
    block_rows = head_rows.shape[0]
    group_width = head_rows.shape[2]
    groups = group_width // HEAD_DIM
    queries = head_rows[:, 0].reshape(block_rows, groups, HEAD_DIM)
    neighbours = padded(head_rows[:, 1:], (("blk", 0),), block_rows)
    key_rows = neighbours[:, 0].reshape(3 * block_rows, groups, HEAD_DIM)
    value_rows = neighbours[:, 1].reshape(3 * block_rows, groups, HEAD_DIM)
    block_index = lax.axis_index("blk")
    labels = jnp.concatenate(
        [
            jnp.full((block_rows,), -1, jnp.int32),
            segments,
            jnp.full((block_rows,), 1073741824, jnp.int32),
        ]
    )
    window_labels = lax.dynamic_slice_in_dim(labels, block_index * block_rows, 3 * block_rows, 0)
    q_labels = lax.dynamic_slice_in_dim(labels, (block_index + 1) * block_rows, block_rows, 0)
    attended, log_sums = attend_forward(queries, key_rows, value_rows, q_labels, window_labels)
    attended_low = attended.astype(jnp.bfloat16).reshape(block_rows, group_width)
    attended_seq = lax.all_to_all(attended_low, "head", split_axis=0, concat_axis=1, tiled=True)
    first_sum = (
        inputs.astype(jnp.float32)
        + jnp.dot(attended_seq, g_out, preferred_element_type=jnp.float32)
        + g_out_bias.astype(jnp.float32)
    )
    normed, ln1_pull = jax.vjp(
        layer_norm, first_sum, g_ln1_gain.astype(jnp.float32), g_ln1_bias.astype(jnp.float32)
    )
    normed_low = normed.astype(jnp.bfloat16)
    hidden_pre = jnp.dot(normed_low, g_in, preferred_element_type=jnp.float32) + g_in_bias.astype(
        jnp.float32
    )
    gelu_value, gelu_pull = jax.vjp(gelu_exact, hidden_pre)
    activated = gelu_value.astype(jnp.bfloat16)
    second_sum = (
        normed
        + jnp.dot(activated, g_down, preferred_element_type=jnp.float32)
        + g_down_bias.astype(jnp.float32)
    )
    outputs, ln2_pull = jax.vjp(
        layer_norm, second_sum, g_ln2_gain.astype(jnp.float32), g_ln2_bias.astype(jnp.float32)
    )
    tied = lax.optimization_barrier((w_qkv, w_out, w_in, w_down, second_sum))
    b_qkv, b_out, b_in, b_down = (
        lax.all_gather(tied[0], ("blk", "head"), axis=0, tiled=True),
        lax.all_gather(tied[1], ("blk", "head"), axis=0, tiled=True),
        lax.all_gather(tied[2], ("blk", "head"), axis=0, tiled=True),
        lax.all_gather(tied[3], ("blk", "head"), axis=0, tiled=True),
    )
    d_second, d_ln2_gain, d_ln2_bias = ln2_pull(cotangent.astype(jnp.float32))
    e_second = d_second.astype(jnp.bfloat16)
    d_down_bias = jnp.sum(e_second.astype(jnp.float32), axis=0)
    d_w_down = jnp.dot(activated.T, e_second, preferred_element_type=jnp.float32)
    d_activated = jnp.dot(e_second, b_down.T, preferred_element_type=jnp.float32)
    d_hidden = gelu_pull(d_activated)[0].astype(jnp.bfloat16)
    d_in_bias = jnp.sum(d_hidden.astype(jnp.float32), axis=0)
    d_w_in = jnp.dot(normed_low.T, d_hidden, preferred_element_type=jnp.float32)
    d_normed = d_second + jnp.dot(d_hidden, b_in.T, preferred_element_type=jnp.float32)
    d_first, d_ln1_gain, d_ln1_bias = ln1_pull(d_normed)
    e_first = d_first.astype(jnp.bfloat16)
    d_out_bias = jnp.sum(e_first.astype(jnp.float32), axis=0)
    d_w_out = jnp.dot(attended_seq.T, e_first, preferred_element_type=jnp.float32)
    d_attended_seq = jnp.dot(e_first, b_out.T, preferred_element_type=jnp.float32).astype(
        jnp.bfloat16
    )
    d_attended = lax.all_to_all(
        d_attended_seq, "head", split_axis=1, concat_axis=0, tiled=True
    ).reshape(block_rows, groups, HEAD_DIM)
    d_queries, d_window = attend_backward(
        queries, key_rows, value_rows, q_labels, window_labels, attended, log_sums, d_attended
    )
    window_flat = d_window.reshape(3 * block_rows, 2, group_width)
    from_next = from_behind(window_flat[:block_rows].astype(jnp.bfloat16), "blk", -1).astype(
        jnp.float32
    )
    from_prev = from_behind(window_flat[2 * block_rows :].astype(jnp.bfloat16), "blk", 1).astype(
        jnp.float32
    )
    d_key_value = window_flat[block_rows : 2 * block_rows] + from_next + from_prev
    d_heads = jnp.concatenate(
        [d_queries.reshape(block_rows, 1, group_width), d_key_value], axis=1
    ).astype(jnp.bfloat16)
    d_qkv = lax.all_to_all(d_heads, "head", split_axis=0, concat_axis=2, tiled=True).reshape(
        tok_rows, 3 * model_width
    )
    d_q_bias = jnp.sum(d_qkv[:, :model_width].astype(jnp.float32), axis=0)
    d_v_bias = jnp.sum(d_qkv[:, 2 * model_width :].astype(jnp.float32), axis=0)
    d_w_qkv = jnp.dot(inputs.T, d_qkv, preferred_element_type=jnp.float32)
    d_inputs = (d_first + jnp.dot(d_qkv, b_qkv.T, preferred_element_type=jnp.float32)).astype(
        jnp.bfloat16
    )
    summed = (
        lax.psum_scatter(d_w_qkv, ("blk", "head"), scatter_dimension=0, tiled=True),
        lax.psum_scatter(d_q_bias, ("blk", "head"), scatter_dimension=0, tiled=True),
        lax.psum_scatter(d_v_bias, ("blk", "head"), scatter_dimension=0, tiled=True),
        lax.psum_scatter(d_w_out, ("blk", "head"), scatter_dimension=0, tiled=True),
        lax.psum_scatter(d_out_bias, ("blk", "head"), scatter_dimension=0, tiled=True),
        lax.psum_scatter(d_ln1_gain, ("blk", "head"), scatter_dimension=0, tiled=True),
        lax.psum_scatter(d_ln1_bias, ("blk", "head"), scatter_dimension=0, tiled=True),
        lax.psum_scatter(d_w_in, ("blk", "head"), scatter_dimension=0, tiled=True),
        lax.psum_scatter(d_in_bias, ("blk", "head"), scatter_dimension=0, tiled=True),
        lax.psum_scatter(d_w_down, ("blk", "head"), scatter_dimension=0, tiled=True),
        lax.psum_scatter(d_down_bias, ("blk", "head"), scatter_dimension=0, tiled=True),
        lax.psum_scatter(d_ln2_gain, ("blk", "head"), scatter_dimension=0, tiled=True),
        lax.psum_scatter(d_ln2_bias, ("blk", "head"), scatter_dimension=0, tiled=True),
    )
    return (
        outputs.astype(jnp.bfloat16),
        d_inputs,
        summed[0],
        summed[1],
        summed[2],
        summed[3],
        summed[4],
        summed[5],
        summed[6],
        summed[7],
        summed[8],
        summed[9],
        summed[10],
        summed[11],
        summed[12],
    )


def solution(mesh):
    placed = (
        P(("blk", "head"), None),
        P(),
        P(("blk", "head"), None),
        P(("blk", "head"), None),
        P(("blk", "head")),
        P(("blk", "head")),
        P(("blk", "head"), None),
        P(("blk", "head")),
        P(("blk", "head")),
        P(("blk", "head")),
        P(("blk", "head"), None),
        P(("blk", "head")),
        P(("blk", "head"), None),
        P(("blk", "head")),
        P(("blk", "head")),
        P(("blk", "head")),
    )
    return jax.shard_map(
        body,
        mesh=mesh,
        in_specs=placed,
        out_specs=(
            P(("blk", "head"), None),
            P(("blk", "head"), None),
            P(("blk", "head"), None),
            P(("blk", "head")),
            P(("blk", "head")),
            P(("blk", "head"), None),
            P(("blk", "head")),
            P(("blk", "head")),
            P(("blk", "head")),
            P(("blk", "head"), None),
            P(("blk", "head")),
            P(("blk", "head"), None),
            P(("blk", "head")),
            P(("blk", "head")),
            P(("blk", "head")),
        ),
        check_vma=False,
    )
```

profile of v0, /device:TPU:0, one launch (start us, length us, event | category | flops | bytes accessed | tf_op | source)
XLA Modules:
  0.0 1307.4 jit_solution(3852219602649752765)
XLA Ops:
  17.0 42.8 %all-reduce.19 = (bf16[768]{0:T(1024)(128)(2,1)S(1)}, bf16[768]{0:T(1024)(128)(2,1)S(1)}, bf16[768]{0:T(1024)(128)(2,1)S(1)}, bf16[768]{0:T(1024)(128)(2,1)S(1)}...) all-reduce(bf16[768]{0:T(1024)(128)(2,1)S(1)} %dynamic-update-slice, ...), channel_id=1, replica_groups=mesh['blk'=8,'head'=4] {'blk','head'}, use_global_device_ids=true, to_apply=%add.1 | all-reduce | flops 9216 | bytes 36864
  84.3 42.1 %all_to_all.68 = bf16[512,3,768]{0,1,2:T(4,128)(2,1)S(1)} all-to-all(bf16[512,3,768]{0,1,2:T(4,128)(2,1)S(1)} %copy.85), channel_id=1, replica_groups=mesh['blk'=8,'head'=4] {'head'}, dimensions={2} | all-to-all | bytes 4718592 | tf_op jit(solution)/shard_map/all_to_all | solution.py:253
  135.7 69.2 %collective-permute-done = bf16[2048,2,192]{0,2,1:T(8,128)(2,1)} collective-permute-done((bf16[2048,2,192]{0,2,1:T(8,128)(2,1)}, bf16[2048,2,192]{0,2,1:T(8,128)(2,1)}, u32[]{:S(2)}, u32[]{:S(2)}) %collective-permute-start) | collective-permute-done | bytes 1572896 | tf_op jit(solution)/shard_map/ppermute | solution.py:14
  211.3 207.1 %while.120 = (s32[]{:T(128)}, f32[2048,3,64]{0,2,1:T(8,128)}, f32[3,2048]{1,0:T(4,128)S(1)}, bf16[2048,3,64]{0,2,1:T(8,128)(2,1)}, s32[2048]{0:T(1024)S(1)}, /*i...) while((s32[]{:T(128)}, f32[2048,3,64]{0,2,1:T(8,128)}, ...), condition=%wide.region_7.8_spmd, body=%wide.region_0.7_spmd.sunk | while | flops 311370752 | bytes 10692945 | solution.py:119
  213.0 26.0 %while.123 = (s32[]{:T(128)}, f32[3,512]{1,0:T(4,128)S(1)}, f32[3,512]{1,0:T(4,128)S(1)}, s32[512]{0:T(512)S(1)}, s32[]{:T(128)}, /*index=5*/s32[6144]{0:T(1024)...) while((s32[]{:T(128)}, f32[3,512]{1,0:T(4,128)S(1)}, ...), condition=%wide.region_4.4_spmd.clone, body=%wide.region_1.3_spmd.clone.sunk | while | flops 106438152 | bytes 7559362 | solution.py:56
  239.0 23.3 %while.124 = (s32[]{:T(128)}, f32[512,3,64]{0,2,1:T(8,128)S(1)}, s32[]{:T(128)}, bf16[6144,3,64]{0,2,1:T(8,128)(2,1)}, s32[512]{0:T(512)S(1)}, /*index=5*/s32[61...) while((s32[]{:T(128)}, f32[512,3,64]{0,2,1:T(8,128)S(1)}, ...), condition=%wide.region_6.6_spmd.clone, body=%wide.region_5.5_spmd.clone.sunk | while | flops 204931072 | bytes 1916612 | solution.py:56
  264.8 26.0 %while.123 = (s32[]{:T(128)}, f32[3,512]{1,0:T(4,128)S(1)}, f32[3,512]{1,0:T(4,128)S(1)}, s32[512]{0:T(512)S(1)}, s32[]{:T(128)}, /*index=5*/s32[6144]{0:T(1024)...) while((s32[]{:T(128)}, f32[3,512]{1,0:T(4,128)S(1)}, ...), condition=%wide.region_4.4_spmd.clone, body=%wide.region_1.3_spmd.clone.sunk | while | flops 106438152 | bytes 7559362 | solution.py:56
  316.6 25.9 %while.123 = (s32[]{:T(128)}, f32[3,512]{1,0:T(4,128)S(1)}, f32[3,512]{1,0:T(4,128)S(1)}, s32[512]{0:T(512)S(1)}, s32[]{:T(128)}, /*index=5*/s32[6144]{0:T(1024)...) while((s32[]{:T(128)}, f32[3,512]{1,0:T(4,128)S(1)}, ...), condition=%wide.region_4.4_spmd.clone, body=%wide.region_1.3_spmd.clone.sunk | while | flops 106438152 | bytes 7559362 | solution.py:56
  342.6 23.3 %while.124 = (s32[]{:T(128)}, f32[512,3,64]{0,2,1:T(8,128)S(1)}, s32[]{:T(128)}, bf16[6144,3,64]{0,2,1:T(8,128)(2,1)}, s32[512]{0:T(512)S(1)}, /*index=5*/s32[61...) while((s32[]{:T(128)}, f32[512,3,64]{0,2,1:T(8,128)S(1)}, ...), condition=%wide.region_6.6_spmd.clone, body=%wide.region_5.5_spmd.clone.sunk | while | flops 204931072 | bytes 1916612 | solution.py:56
  368.3 25.9 %while.123 = (s32[]{:T(128)}, f32[3,512]{1,0:T(4,128)S(1)}, f32[3,512]{1,0:T(4,128)S(1)}, s32[512]{0:T(512)S(1)}, s32[]{:T(128)}, /*index=5*/s32[6144]{0:T(1024)...) while((s32[]{:T(128)}, f32[3,512]{1,0:T(4,128)S(1)}, ...), condition=%wide.region_4.4_spmd.clone, body=%wide.region_1.3_spmd.clone.sunk | while | flops 106438152 | bytes 7559362 | solution.py:56
  394.3 23.3 %while.124 = (s32[]{:T(128)}, f32[512,3,64]{0,2,1:T(8,128)S(1)}, s32[]{:T(128)}, bf16[6144,3,64]{0,2,1:T(8,128)(2,1)}, s32[512]{0:T(512)S(1)}, /*index=5*/s32[61...) while((s32[]{:T(128)}, f32[512,3,64]{0,2,1:T(8,128)S(1)}, ...), condition=%wide.region_6.6_spmd.clone, body=%wide.region_5.5_spmd.clone.sunk | while | flops 204931072 | bytes 1916612 | solution.py:56
  475.0 53.9 %all-gather.17.cloned.1.call-done = bf16[3072,768]{1,0:T(8,128)(2,1)} async-done(((bf16[96,768]{1,0:T(8,128)(2,1)}), bf16[3072,768]{1,0:T(8,128)(2,1)}) %all-gather.17.cloned.1.call-update) | async-done | bytes 4718608 | tf_op jit(solution)/shard_map/all_gather | solution.py:301
  541.9 52.1 %all-gather.19.cloned.1.call-done = bf16[768,3072]{1,0:T(8,128)(2,1)} async-done(((bf16[24,3072]{1,0:T(8,128)(2,1)}), bf16[768,3072]{1,0:T(8,128)(2,1)}) %all-gather.19.cloned.1.call-update) | async-done | bytes 4718608 | tf_op jit(solution)/shard_map/all_gather | solution.py:300
  615.3 34.6 %all-gather.21.cloned.1.call-done = bf16[768,768]{1,0:T(8,128)(2,1)} async-done(((bf16[24,768]{1,0:T(8,128)(2,1)}), bf16[768,768]{1,0:T(8,128)(2,1)}) %all-gather.21.cloned.1.call-update) | async-done | bytes 1179664 | tf_op jit(solution)/shard_map/all_gather | solution.py:299
  675.0 336.3 %while.122 = (s32[]{:T(128)}, bf16[2048,3,64]{0,2,1:T(8,128)(2,1)}, f32[6144,2,3,64]{0,3,2,1:T(8,128)}, bf16[2048,3,64]{0,2,1:T(8,128)(2,1)}, s32[2048]{0:T(1024...) while((s32[]{:T(128)}, bf16[2048,3,64]{0,2,1:T(8,128)(2,1)}, ...), condition=%wide.region_20.21_spmd, body=%wide.region_16.20_spmd.sunk | while | flops 512522752 | bytes 22463076 | solution.py:189
  677.2 81.1 %while.125 = (s32[]{:T(128)}, f32[512,3,64]{0,2,1:T(8,128)S(1)}, f32[6144,2,3,64]{0,3,2,1:T(8,128)}, s32[]{:T(128)}, bf16[6144,3,64]{0,2,1:T(8,128)(2,1)}, /*ind...) while((s32[]{:T(128)}, f32[512,3,64]{0,2,1:T(8,128)S(1)}, ...), condition=%wide.region_19.19_spmd.clone, body=%wide.region_18.18_spmd.clone.sunk | while | flops 512229376 | bytes 20277484 | solution.py:56
  761.2 81.1 %while.125 = (s32[]{:T(128)}, f32[512,3,64]{0,2,1:T(8,128)S(1)}, f32[6144,2,3,64]{0,3,2,1:T(8,128)}, s32[]{:T(128)}, bf16[6144,3,64]{0,2,1:T(8,128)(2,1)}, /*ind...) while((s32[]{:T(128)}, f32[512,3,64]{0,2,1:T(8,128)S(1)}, ...), condition=%wide.region_19.19_spmd.clone, body=%wide.region_18.18_spmd.clone.sunk | while | flops 512229376 | bytes 20277484 | solution.py:56
  845.2 81.2 %while.125 = (s32[]{:T(128)}, f32[512,3,64]{0,2,1:T(8,128)S(1)}, f32[6144,2,3,64]{0,3,2,1:T(8,128)}, s32[]{:T(128)}, bf16[6144,3,64]{0,2,1:T(8,128)(2,1)}, /*ind...) while((s32[]{:T(128)}, f32[512,3,64]{0,2,1:T(8,128)S(1)}, ...), condition=%wide.region_19.19_spmd.clone, body=%wide.region_18.18_spmd.clone.sunk | while | flops 512229376 | bytes 20277484 | solution.py:56
  929.3 81.3 %while.125 = (s32[]{:T(128)}, f32[512,3,64]{0,2,1:T(8,128)S(1)}, f32[6144,2,3,64]{0,3,2,1:T(8,128)}, s32[]{:T(128)}, bf16[6144,3,64]{0,2,1:T(8,128)(2,1)}, /*ind...) while((s32[]{:T(128)}, f32[512,3,64]{0,2,1:T(8,128)S(1)}, ...), condition=%wide.region_19.19_spmd.clone, body=%wide.region_18.18_spmd.clone.sunk | while | flops 512229376 | bytes 20277484 | solution.py:56
  1024.5 43.2 %collective-permute-done.2 = bf16[2048,2,192]{0,2,1:T(8,128)(2,1)S(1)} collective-permute-done((bf16[2048,2,192]{0,2,1:T(8,128)(2,1)S(1)}, bf16[2048,2,192]{0,2,1:T(8,128)(2,1)S(1)}, u32[]{:S(2)}, u32[]{:S(2)}) %collective-permute-start.2) | collective-permute-done | bytes 1572896 | tf_op jit(solution)/shard_map/ppermute | solution.py:25
  1067.7 31.5 %collective-permute-done.3 = bf16[2048,2,192]{0,2,1:T(8,128)(2,1)S(1)} collective-permute-done((bf16[2048,2,192]{0,2,1:T(8,128)(2,1)S(1)}, bf16[2048,2,192]{0,2,1:T(8,128)(2,1)S(1)}, u32[]{:S(2)}, u32[]{:S(2)}) %collective-permute-start.3) | collective-permute-done | bytes 1572896 | tf_op jit(solution)/shard_map/ppermute | solution.py:25
  1105.0 56.2 %all_to_all.69 = bf16[2048,3,192]{2,1,0:T(4,128)(2,1)} all-to-all(bf16[2048,3,192]{2,1,0:T(4,128)(2,1)} %copy.91), channel_id=1, replica_groups=mesh['blk'=8,'head'=4] {'head'}, dimensions={0} | all-to-all | bytes 4718592 | tf_op jit(solution)/shard_map/all_to_all | solution.py:336
  1180.3 42.2 %all-reduce.18 = (f32[768]{0:T(1024)S(1)}, f32[768]{0:T(1024)S(1)}, f32[768]{0:T(1024)S(1)}, f32[768]{0:T(1024)S(1)}, f32[768]{0:T(1024)S(1)}, /*index=5*/f32[30...) all-reduce(f32[768]{0:T(1024)S(1)} %get-tuple-element.1126, ...), channel_id=3, replica_groups=mesh['blk'=8,'head'=4] {'blk','head'}, use_global_device_ids=true, to_apply=%region_23.24.clone | all-reduce | flops 9216 | bytes 73728
  1233.2 66.9 %reduce-scatter.13.cloned.1.call-done = f32[24,2304]{1,0:T(8,128)} async-done(((f32[768,2304]{1,0:T(8,128)}), f32[24,2304]{1,0:T(8,128)}) %reduce-scatter.13.cloned.1.call-update) | async-done | bytes 221200
  (881 shorter events, 774.8 us)
Async XLA Ops:
  7.2 66.6 %all-gather.9.cloned.1.call-start = ((), (), s32[]{:S(2)}) async-start(), calls=%async_computation.8 | async-start | bytes 3649536 | tf_op jit(solution)/shard_map/all_gather | solution.py:211
  7.9 417.7 %all-gather.11.cloned.1.call-start = ((), (), s32[]{:S(2)}) async-start(), calls=%async_computation.9 | async-start | bytes 1216512 | tf_op jit(solution)/shard_map/all_gather | solution.py:214
  8.7 431.0 %all-gather.13.cloned.1.call-start = ((), (), s32[]{:S(2)}) async-start(), calls=%async_computation.10 | async-start | bytes 4866048 | tf_op jit(solution)/shard_map/all_gather | solution.py:218
  9.4 449.9 %all-gather.15.cloned.1.call-start = ((), (), s32[]{:S(2)}) async-start(), calls=%async_computation.11 | async-start | bytes 4866048 | tf_op jit(solution)/shard_map/all_gather | solution.py:220
  127.0 7.6 copy-start.9
  128.6 76.3 %collective-permute-start = (bf16[2048,2,192]{0,2,1:T(8,128)(2,1)}, bf16[2048,2,192]{0,2,1:T(8,128)(2,1)}, u32[]{:S(2)}, u32[]{:S(2)}) collective-permute-start(bf16[2048,2,192]{0,2,1:T(8,128)(2,1)} %slice.45), channel_id=1, source_target_pairs={{0,4},{4,8},{8,12},{12,16},{16,20},{20,24},{24,28},{1,5},{5,9},{9,... | collective-permute-start | bytes 4718600 | tf_op jit(solution)/shard_map/ppermute | solution.py:14
  133.0 71.8 %collective-permute-start.1 = (bf16[2048,2,192]{0,2,1:T(8,128)(2,1)}, bf16[2048,2,192]{0,2,1:T(8,128)(2,1)}, u32[]{:S(2)}, u32[]{:S(2)}) collective-permute-start(bf16[2048,2,192]{0,2,1:T(8,128)(2,1)} %slice.45), channel_id=1, source_target_pairs={{4,0},{8,4},{12,8},{16,12},{20,16},{24,20},{28,24},{5,1},{9,5},{13... | collective-permute-start | bytes 4718600 | tf_op jit(solution)/shard_map/ppermute | solution.py:17
  421.5 15.1 %all-to-all-start.1 = ((bf16[4,512,192]{1,2,0:T(8,128)(2,1)}), bf16[4,512,192]{1,2,0:T(8,128)(2,1)S(1)}, u32[]{:S(2)}, u32[]{:S(2)}) async-start(bf16[4,512,192]{1,2,0:T(8,128)(2,1)} %copy.88), calls=%async_computation.1 | async-start | bytes 1572864 | tf_op jit(solution)/shard_map/all_to_all | solution.py:273
  425.0 103.9 %all-gather.17.cloned.1.call-start = ((), (), s32[]{:S(2)}) async-start(), calls=%async_computation.12 | async-start | bytes 4866048 | tf_op jit(solution)/shard_map/all_gather | solution.py:301
  459.3 8.4 copy-start.20
  459.3 8.4 copy-start.19
  465.4 128.6 %all-gather.19.cloned.1.call-start = ((), (), s32[]{:S(2)}) async-start(), calls=%async_computation.13 | async-start | bytes 4866048 | tf_op jit(solution)/shard_map/all_gather | solution.py:300
  466.0 183.9 %all-gather.21.cloned.1.call-start = ((), (), s32[]{:S(2)}) async-start(), calls=%async_computation.14 | async-start | bytes 1216512 | tf_op jit(solution)/shard_map/all_gather | solution.py:299
  466.7 761.0 %all-gather.23.cloned.1.call-start = ((), (), s32[]{:S(2)}) async-start(), calls=%async_computation.15 | async-start | bytes 3649536 | tf_op jit(solution)/shard_map/all_gather | solution.py:298
  467.5 765.7 %reduce-scatter.7.cloned.1.call-start = ((), (), s32[]{:S(2)}) async-start(), calls=%async_computation.16 | async-start | bytes 2433024 | tf_op jit(solution)/shard_map/reduce_scatter | solution.py:349
  528.8 65.2 %copy-start.2 = (f32[512,768]{1,0:T(8,128)S(1)}, f32[512,768]{1,0:T(8,128)}, u32[]{:S(2)}) copy-start(f32[512,768]{1,0:T(8,128)} %copy-done.1) | copy-start | bytes 4718596
  605.8 627.4 %reduce-scatter.11.cloned.1.call-start = ((), (), s32[]{:S(2)}) async-start(), calls=%async_computation.18 | async-start | bytes 9732096 | tf_op jit(solution)/shard_map/reduce_scatter | solution.py:355
  653.1 15.9 %all-to-all-start.2 = ((bf16[512,4,192]{0,2,1:T(8,128)(2,1)}), bf16[512,4,192]{0,2,1:T(8,128)(2,1)S(1)}, u32[]{:S(2)}, u32[]{:S(2)}) async-start(bf16[512,4,192]{0,2,1:T(8,128)(2,1)} %bitcast.9), calls=%async_computation.2 | async-start | bytes 1572864 | tf_op jit(solution)/shard_map/all_to_all | solution.py:319
  656.6 576.6 %reduce-scatter.9.cloned.1.call-start = ((), (), s32[]{:S(2)}) async-start(), calls=%async_computation.17 | async-start | bytes 9732096 | tf_op jit(solution)/shard_map/reduce_scatter | solution.py:353
  663.8 636.2 %reduce-scatter.13.cloned.1.call-start = ((), (), s32[]{:S(2)}) async-start(), calls=%async_computation.19 | async-start | bytes 7299072
  1016.0 51.7 %collective-permute-start.2 = (bf16[2048,2,192]{0,2,1:T(8,128)(2,1)S(1)}, bf16[2048,2,192]{0,2,1:T(8,128)(2,1)S(1)}, u32[]{:S(2)}, u32[]{:S(2)}) collective-permute-start(bf16[2048,2,192]{0,2,1:T(8,128)(2,1)S(1)} %bitcast.168), channel_id=1, source_target_pairs={{4,0},{8,4},{12,8},{16,12},{20,16},{24,20},{28,24},{5,1},{9,5},{13... | collective-permute-start | bytes 4718600 | tf_op jit(solution)/shard_map/ppermute | solution.py:25
  1017.3 81.9 %collective-permute-start.3 = (bf16[2048,2,192]{0,2,1:T(8,128)(2,1)S(1)}, bf16[2048,2,192]{0,2,1:T(8,128)(2,1)S(1)}, u32[]{:S(2)}, u32[]{:S(2)}) collective-permute-start(bf16[2048,2,192]{0,2,1:T(8,128)(2,1)S(1)} %bitcast.167), channel_id=1, source_target_pairs={{0,4},{4,8},{8,12},{12,16},{16,20},{20,24},{24,28},{1,5},{5,9},{9,... | collective-permute-start | bytes 4718600 | tf_op jit(solution)/shard_map/ppermute | solution.py:25
  1024.5 75.5 %copy-start.3 = (bf16[2048,3,64]{0,2,1:T(8,128)(2,1)S(1)}, bf16[2048,3,64]{0,2,1:T(8,128)(2,1)}, u32[]{:S(2)}) copy-start(bf16[2048,3,64]{0,2,1:T(8,128)(2,1)} %get-tuple-element.915) | copy-start | bytes 2359300
  1179.6 48.1 %copy-start.16 = (f32[512]{0:T(512)S(1)}, f32[512]{0:T(512)}, u32[]{:S(2)}) copy-start(f32[512]{0:T(512)} %copy-done.15) | copy-start | bytes 6148
  (15 other events, 27.8 us)
Sparse Core Ops, SparseCore 0:
  10.9 62.8 all-gather.8
  76.7 54.4 all-gather.10
  134.1 90.5 all-gather.12
  227.4 62.8 all-gather.14
  465.5 63.2 all-gather.16
  531.6 62.3 all-gather.18
  596.9 52.8 all-gather.20
  652.8 59.0 all-gather.22
  717.7 97.7 reduce-scatter.6
  822.8 134.8 reduce-scatter.10
  964.2 180.1 reduce-scatter.8
  1179.8 120.2 reduce-scatter.12
where the time goes:
time: 1320 us; the launch traced here: 1310 us
  matrix products  462 us (35%)
  waiting for transfers between devices  386 us (29%)
  blocking collectives  183 us (14%)
  other arithmetic  152 us (12%)
  local copies, waits for them, and re-layouts  82.7 us (6%)
  starting transfers between devices  20.6 us (2%)
  between operations  15.2 us (1%)
    dot_general x72, matrix products, doc_scores(): jnp.einsum('qhd,khd->hqk', q_tile, k_tile, preferred_element_type=jnp.flo...  121 us
    unnamed x2, blocking collectives  85 us
    dot_general x36, matrix products, add_values(): jnp.einsum('hqk,khd->qhd', softmax_w, v_tile, preferred_element_type=jnp....  80.8 us
    dynamic_update_slice x36, other arithmetic, grads_step(): lax.dynamic_update_slice_in_dim(window_grads, current + key_value_part, k...  80.1 us
    dot_general x36, matrix products, grads_step(): jnp.einsum('qhd,khd->hqk', do_tile, v_tile, preferred_element_type=jnp.fl...  77.9 us
    ppermute x2, waiting for transfers between devices, from_behind(): lax.ppermute(value, axis, [(source, source + steps) for source in range(f...  74.7 us
    unnamed x13, waiting for transfers between devices  71 us
    ppermute x1, waiting for transfers between devices, padded(): lax.ppermute(lax.slice_in_dim(block, block.shape[dim] - width, None, axis...  69.2 us
  transfers between devices with their start and end apart: 18, of which 10 were waited for; matrix products, arithmetic and copies ran while one was open for 53% of the time, Pallas kernels for 0%

commit v1 on v0

v1 whole, which is shorter than its diff:
```python
import functools

import jax
import jax.numpy as jnp
from jax import lax
from jax.experimental import pallas as pl
from jax.experimental.pallas import tpu as pltpu
from jax.sharding import PartitionSpec as P

HEAD_DIM = 64
HD = 64


def padded(block, sides, width):
    for axis, dim in sides:
        count = lax.axis_size(axis)
        forward = [(i, i + 1) for i in range(count - 1)]
        backward = [(target, source) for source, target in forward]
        low = lax.ppermute(
            lax.slice_in_dim(block, block.shape[dim] - width, None, axis=dim), axis, forward
        )
        high = lax.ppermute(lax.slice_in_dim(block, 0, width, axis=dim), axis, backward)
        block = jnp.concatenate([low, block, high], axis=dim)
    return block


def from_behind(value, axis, steps):
    count = lax.axis_size(axis)
    first, last = (max(0, -steps), min(count, count - steps))
    return lax.ppermute(value, axis, [(source, source + steps) for source in range(first, last)])


def layer_norm(values, gain, shift_vec):
    centre = jnp.mean(values, axis=-1, keepdims=True)
    centered = values - centre
    spread = jnp.mean(centered * centered, axis=-1, keepdims=True)
    return centered * lax.rsqrt(spread + 1e-05) * gain + shift_vec


def gelu_exact(values):
    return jax.nn.gelu(values, approximate=False)


F32=jnp.float32; BF=jnp.bfloat16
NEG=-1e30

def dot(a,b): return jnp.dot(a,b,preferred_element_type=F32)

def fwd_body(lo_ref,hi_ref,qT_ref,k_ref,vT_ref,qs_ref,qe_ref,oT_ref,lse_ref,*,TQ,TK,H):
    nq=qT_ref.shape[2]//TQ
    def qloop(i,_):
        qsl=pl.ds(pl.multiple_of(i*TQ,TQ),TQ)
        qs=qs_ref[:,qsl]; qe=qe_ref[:,qsl]
        qts=[qT_ref[h,:,qsl]*BF(HD**-0.5) for h in range(H)]
        def kloop(j,c):
            ksl=pl.ds(pl.multiple_of(j*TK,TK),TK)
            pos=lax.broadcasted_iota(jnp.int32,(TK,TQ),0)+j*TK
            mask=(pos>=qs)&(pos<qe)
            out=[]
            for h in range(H):
                m,l,acc=c[h]
                s=jnp.where(mask,dot(k_ref[h,ksl,:],qts[h]),NEG)
                mn=jnp.maximum(m,jnp.max(s,axis=0,keepdims=True))
                p=jnp.exp(s-mn)
                al=jnp.exp(m-mn)
                l=l*al+jnp.sum(p,axis=0,keepdims=True)
                acc=acc*al+dot(vT_ref[h,:,ksl],p.astype(BF))
                out.append((mn,l,acc))
            return tuple(out)
        init=tuple((jnp.full((1,TQ),NEG,F32),jnp.zeros((1,TQ),F32),jnp.zeros((HD,TQ),F32)) for _ in range(H))
        res=lax.fori_loop(lo_ref[i],hi_ref[i],kloop,init)
        for h in range(H):
            m,l,acc=res[h]
            oT_ref[h,:,qsl]=acc/l
            lse_ref[h:h+1,qsl]=m+jnp.log(l)
        return 0
    lax.fori_loop(0,nq,qloop,0)

def attn_fwd(qT,k,vT,lo,hi,qs,qe,TQ=256,TK=256):
    H,_,N=qT.shape
    V=pl.BlockSpec(memory_space=pltpu.VMEM); S=pl.BlockSpec(memory_space=pltpu.SMEM)
    return pl.pallas_call(functools.partial(fwd_body,TQ=TQ,TK=TK,H=H),
        out_shape=(jax.ShapeDtypeStruct((H,HD,N),F32),jax.ShapeDtypeStruct((H,N),F32)),
        in_specs=[S,S,V,V,V,V,V],out_specs=(V,V),
        compiler_params=pltpu.CompilerParams(vmem_limit_bytes=48<<20),name="attn_fwd",
        cost_estimate=pl.CostEstimate(flops=int(4e9),bytes_accessed=int(2e7),transcendentals=int(1.5e7)))(lo,hi,qT,k,vT,qs,qe)

def bwdA_body(lo_ref,hi_ref,qT_ref,q_ref,doT_ref,do_ref,lse_ref,dl_ref,k_ref,kT_ref,v_ref,qs_ref,qe_ref,
              dqT_ref,dk_ref,dv_ref,*,T,H,nb):
    dqT_ref[...]=jnp.zeros_like(dqT_ref)
    dk_ref[...]=jnp.zeros_like(dk_ref)
    dv_ref[...]=jnp.zeros_like(dv_ref)
    def qloop(i,_):
        qsl=pl.ds(pl.multiple_of(i*T,T),T)
        qs=qs_ref[:,qsl]; qe=qe_ref[:,qsl]
        def pair(j,own):
            ksl=pl.ds(pl.multiple_of(j*T,T),T)
            osl=pl.ds(pl.multiple_of((j-nb)*T,T),T)
            pos=lax.broadcasted_iota(jnp.int32,(T,T),0)+j*T
            mask=(pos>=qs)&(pos<qe)
            for h in range(H):
                qT=qT_ref[h,:,qsl]*BF(HD**-0.5)
                s=dot(k_ref[h,ksl,:],qT)
                p=jnp.where(mask,jnp.exp(s-lse_ref[h:h+1,qsl]),0.0)
                dp=dot(v_ref[h,ksl,:],doT_ref[h,:,qsl])
                ds=(p*(dp-dl_ref[h:h+1,qsl])).astype(BF)
                dqT_ref[h,:,qsl]+=dot(kT_ref[h,:,ksl],ds)
                if own:
                    dv_ref[h,osl,:]+=dot(p.astype(BF),do_ref[h,qsl,:])
                    dk_ref[h,osl,:]+=dot(ds,q_ref[h,qsl,:])
        lo=lo_ref[i]; hi=hi_ref[i]
        lax.fori_loop(jnp.maximum(lo,nb),jnp.minimum(hi,2*nb),lambda j,_:(pair(j,True),0)[1],0)
        lax.fori_loop(lo,jnp.minimum(hi,nb),lambda j,_:(pair(j,False),0)[1],0)
        lax.fori_loop(jnp.maximum(lo,2*nb),hi,lambda j,_:(pair(j,False),0)[1],0)
        return 0
    lax.fori_loop(0,nb,qloop,0)
    dqT_ref[...]=dqT_ref[...]*(HD**-0.5)

def attn_bwdA(qT,q,doT,do,lse,dl,k,kT,v,lo,hi,qs,qe,T=256):
    H,_,N=qT.shape
    V=pl.BlockSpec(memory_space=pltpu.VMEM); S=pl.BlockSpec(memory_space=pltpu.SMEM)
    return pl.pallas_call(functools.partial(bwdA_body,T=T,H=H,nb=N//T),
        out_shape=(jax.ShapeDtypeStruct((H,HD,N),F32),jax.ShapeDtypeStruct((H,N,HD),F32),jax.ShapeDtypeStruct((H,N,HD),F32)),
        in_specs=[S,S]+[V]*11,out_specs=(V,V,V),
        compiler_params=pltpu.CompilerParams(vmem_limit_bytes=56<<20),name="attn_bwdA",
        cost_estimate=pl.CostEstimate(flops=int(1e10),bytes_accessed=int(4e7),transcendentals=int(1.5e7)))(lo,hi,qT,q,doT,do,lse,dl,k,kT,v,qs,qe)


def bwdB_body(lo_ref,hi_ref,qT_ref,q_ref,doT_ref,do_ref,lse_ref,dl_ref,k_ref,v_ref,dk0_ref,dv0_ref,qs_ref,qe_ref,
              dk_ref,dv_ref,*,T,H,nb):
    dk_ref[...]=dk0_ref[...]
    dv_ref[...]=dv0_ref[...]
    def kloop(j,_):
        osl=pl.ds(pl.multiple_of(j*T,T),T)
        def pair(i):
            qsl=pl.ds(pl.multiple_of(i*T,T),T)
            pos=lax.broadcasted_iota(jnp.int32,(T,T),0)+(j+nb)*T
            mask=(pos>=qs_ref[:,qsl])&(pos<qe_ref[:,qsl])
            for h in range(H):
                qT=qT_ref[h,:,qsl]*BF(HD**-0.5)
                s=dot(k_ref[h,osl,:],qT)
                p=jnp.where(mask,jnp.exp(s-lse_ref[h:h+1,qsl]),0.0)
                dp=dot(v_ref[h,osl,:],doT_ref[h,:,qsl])
                ds=(p*(dp-dl_ref[h:h+1,qsl])).astype(BF)
                dv_ref[h,osl,:]+=dot(p.astype(BF),do_ref[h,qsl,:])
                dk_ref[h,osl,:]+=dot(ds,q_ref[h,qsl,:])
        lo=lo_ref[j]; hi=hi_ref[j]
        lax.fori_loop(lo,jnp.minimum(hi,nb),lambda i,_:(pair(i),0)[1],0)
        lax.fori_loop(jnp.maximum(lo,2*nb),hi,lambda i,_:(pair(i-nb),0)[1],0)
        return 0
    lax.fori_loop(0,nb,kloop,0)
    dk_ref[...]=dk_ref[...]*(HD**-0.5)

def attn_bwdB(qT,q,doT,do,lse,dl,k,v,dk0,dv0,lo,hi,qs,qe,T=256):
    H,N,_=k.shape
    V=pl.BlockSpec(memory_space=pltpu.VMEM); S=pl.BlockSpec(memory_space=pltpu.SMEM)
    return pl.pallas_call(functools.partial(bwdB_body,T=T,H=H,nb=N//T),
        out_shape=(jax.ShapeDtypeStruct((H,N,HD),F32),jax.ShapeDtypeStruct((H,N,HD),F32)),
        in_specs=[S,S]+[V]*12,out_specs=(V,V),
        compiler_params=pltpu.CompilerParams(vmem_limit_bytes=56<<20),name="attn_bwdB",
        cost_estimate=pl.CostEstimate(flops=int(4e9),bytes_accessed=int(4e7),transcendentals=int(5e6)))(lo,hi,qT,q,doT,do,lse,dl,k,v,dk0,dv0,qs,qe)

def tile_ranges(segments, first, block, tile):
    tok=jnp.arange(segments.shape[0],dtype=jnp.int32)
    return tok


def body(
    inputs,
    segments,
    cotangent,
    w_qkv,
    q_bias,
    v_bias,
    w_out,
    out_bias,
    ln1_gain,
    ln1_bias,
    w_in,
    in_bias,
    w_down,
    down_bias,
    ln2_gain,
    ln2_bias,
):
    gathered = (
        lax.all_gather(w_qkv, ("blk", "head"), axis=0, tiled=True),
        lax.all_gather(q_bias, ("blk", "head"), axis=0, tiled=True),
        lax.all_gather(v_bias, ("blk", "head"), axis=0, tiled=True),
        lax.all_gather(w_out, ("blk", "head"), axis=0, tiled=True),
        lax.all_gather(out_bias, ("blk", "head"), axis=0, tiled=True),
        lax.all_gather(ln1_gain, ("blk", "head"), axis=0, tiled=True),
        lax.all_gather(ln1_bias, ("blk", "head"), axis=0, tiled=True),
        lax.all_gather(w_in, ("blk", "head"), axis=0, tiled=True),
        lax.all_gather(in_bias, ("blk", "head"), axis=0, tiled=True),
        lax.all_gather(w_down, ("blk", "head"), axis=0, tiled=True),
        lax.all_gather(down_bias, ("blk", "head"), axis=0, tiled=True),
        lax.all_gather(ln2_gain, ("blk", "head"), axis=0, tiled=True),
        lax.all_gather(ln2_bias, ("blk", "head"), axis=0, tiled=True),
    )
    (
        g_qkv,
        g_q_bias,
        g_v_bias,
        g_out,
        g_out_bias,
        g_ln1_gain,
        g_ln1_bias,
        g_in,
        g_in_bias,
        g_down,
        g_down_bias,
        g_ln2_gain,
        g_ln2_bias,
    ) = gathered
    tok_rows, model_width = inputs.shape
    qkv_bias = jnp.concatenate(
        [
            g_q_bias.astype(jnp.float32),
            jnp.zeros((model_width,), jnp.float32),
            g_v_bias.astype(jnp.float32),
        ]
    )
    mixed_qkv = (
        (jnp.dot(inputs, g_qkv, preferred_element_type=jnp.float32) + qkv_bias)
        .astype(jnp.bfloat16)
        .reshape(tok_rows, 3, model_width)
    )
    head_rows = lax.all_to_all(mixed_qkv, "head", split_axis=2, concat_axis=0, tiled=True)
    block_rows = head_rows.shape[0]
    group_width = head_rows.shape[2]
    groups = group_width // HEAD_DIM
    kv_width = groups
    def heads_of(rows):
        return rows.reshape(rows.shape[0], groups, HEAD_DIM).transpose(1, 0, 2)
    neighbours = padded(head_rows, (("blk", 0),), block_rows)
    q_win, k_win, v_win = (heads_of(neighbours[:, n]) for n in range(3))
    q_own = q_win[:, block_rows : 2 * block_rows]
    swap = lambda a: a.transpose(0, 2, 1)
    block_index = lax.axis_index("blk")
    TILE = 512
    total = segments.shape[0]
    first = (block_index - 1) * block_rows
    padded_seg = jnp.concatenate(
        [jnp.full((block_rows,), -1, jnp.int32), segments, jnp.full((block_rows,), 1 << 30, jnp.int32)]
    )
    win_seg = lax.dynamic_slice_in_dim(padded_seg, block_index * block_rows, 3 * block_rows, 0)
    below = jnp.sum((win_seg[None, :] < win_seg[::TILE][:, None]).astype(jnp.int32), axis=1)
    upto = jnp.sum((win_seg[None, :] <= win_seg[TILE - 1 :: TILE][:, None]).astype(jnp.int32), axis=1)
    pos = jnp.arange(3 * block_rows, dtype=jnp.int32)
    newdoc = jnp.concatenate([jnp.ones((1,), bool), win_seg[1:] != win_seg[:-1]])
    qs = lax.cummax(jnp.where(newdoc, pos, 0))
    enddoc = jnp.concatenate([win_seg[1:] != win_seg[:-1], jnp.ones((1,), bool)])
    qe = lax.cummin(jnp.where(enddoc, pos + 1, 3 * block_rows), reverse=True)
    nb = block_rows // TILE
    t_lo = (below // TILE)[nb : 2 * nb]
    t_hi = ((upto - 1) // TILE + 1)[nb : 2 * nb]
    qs, qe = qs[None], qe[None]
    qs_own, qe_own = (a[:, block_rows : 2 * block_rows] for a in (qs, qe))
    qT_own = swap(q_own)
    oT, lse = attn_fwd(qT_own, k_win, swap(v_win), t_lo, t_hi, qs_own, qe_own, TILE, TILE)
    attended = oT.reshape(group_width, block_rows).T
    attended_low = attended.astype(jnp.bfloat16).reshape(block_rows, group_width)
    attended_seq = lax.all_to_all(attended_low, "head", split_axis=0, concat_axis=1, tiled=True)
    first_sum = (
        inputs.astype(jnp.float32)
        + jnp.dot(attended_seq, g_out, preferred_element_type=jnp.float32)
        + g_out_bias.astype(jnp.float32)
    )
    normed, ln1_pull = jax.vjp(
        layer_norm, first_sum, g_ln1_gain.astype(jnp.float32), g_ln1_bias.astype(jnp.float32)
    )
    normed_low = normed.astype(jnp.bfloat16)
    hidden_pre = jnp.dot(normed_low, g_in, preferred_element_type=jnp.float32) + g_in_bias.astype(
        jnp.float32
    )
    gelu_value, gelu_pull = jax.vjp(gelu_exact, hidden_pre)
    activated = gelu_value.astype(jnp.bfloat16)
    second_sum = (
        normed
        + jnp.dot(activated, g_down, preferred_element_type=jnp.float32)
        + g_down_bias.astype(jnp.float32)
    )
    outputs, ln2_pull = jax.vjp(
        layer_norm, second_sum, g_ln2_gain.astype(jnp.float32), g_ln2_bias.astype(jnp.float32)
    )
    b_qkv, b_out, b_in, b_down = g_qkv, g_out, g_in, g_down
    d_second, d_ln2_gain, d_ln2_bias = ln2_pull(cotangent.astype(jnp.float32))
    e_second = d_second.astype(jnp.bfloat16)
    d_down_bias = jnp.sum(e_second.astype(jnp.float32), axis=0)
    d_w_down = jnp.dot(activated.T, e_second, preferred_element_type=jnp.float32)
    d_activated = jnp.dot(e_second, b_down.T, preferred_element_type=jnp.float32)
    d_hidden = gelu_pull(d_activated)[0].astype(jnp.bfloat16)
    d_in_bias = jnp.sum(d_hidden.astype(jnp.float32), axis=0)
    d_w_in = jnp.dot(normed_low.T, d_hidden, preferred_element_type=jnp.float32)
    d_normed = d_second + jnp.dot(d_hidden, b_in.T, preferred_element_type=jnp.float32)
    d_first, d_ln1_gain, d_ln1_bias = ln1_pull(d_normed)
    e_first = d_first.astype(jnp.bfloat16)
    d_out_bias = jnp.sum(e_first.astype(jnp.float32), axis=0)
    d_w_out = jnp.dot(attended_seq.T, e_first, preferred_element_type=jnp.float32)
    d_attended_seq = jnp.dot(e_first, b_out.T, preferred_element_type=jnp.float32).astype(
        jnp.bfloat16
    )
    d_attended = lax.all_to_all(
        d_attended_seq, "head", split_axis=1, concat_axis=0, tiled=True
    )
    doT = d_attended.T.reshape(groups, HEAD_DIM, block_rows)
    delta = jnp.sum(doT.astype(jnp.float32) * oT, axis=1)
    stats = jnp.concatenate([lse, delta], axis=0).T
    do_win = padded(d_attended, (("blk", 0),), block_rows)
    stats_win = padded(stats, (("blk", 0),), block_rows).T
    do_own = heads_of(d_attended)
    dqT, dk0, dv0 = attn_bwdA(
        qT_own, q_own, doT, do_own, lse, delta, k_win, swap(k_win), v_win, t_lo, t_hi, qs_own, qe_own, TILE
    )
    outer = lambda a, ax: jnp.concatenate(
        [lax.slice_in_dim(a, 0, block_rows, axis=ax), lax.slice_in_dim(a, 2 * block_rows, None, axis=ax)], axis=ax
    )
    do_out = heads_of(outer(do_win, 0))
    q_out = outer(q_win, 1)
    st_out = outer(stats_win, 1)
    dk, dv = attn_bwdB(
        swap(q_out), q_out, swap(do_out), do_out, st_out[:groups], st_out[groups:],
        k_win[:, block_rows : 2 * block_rows], v_win[:, block_rows : 2 * block_rows], dk0, dv0,
        t_lo, t_hi, outer(qs, 1), outer(qe, 1), TILE
    )
    rows_of = lambda a: a.astype(jnp.bfloat16).transpose(1, 0, 2).reshape(block_rows, group_width)
    d_heads = jnp.stack([dqT.astype(jnp.bfloat16).reshape(group_width, block_rows).T, rows_of(dk), rows_of(dv)], axis=1)
    d_qkv = lax.all_to_all(d_heads, "head", split_axis=0, concat_axis=2, tiled=True).reshape(
        tok_rows, 3 * model_width
    )
    d_q_bias = jnp.sum(d_qkv[:, :model_width].astype(jnp.float32), axis=0)
    d_v_bias = jnp.sum(d_qkv[:, 2 * model_width :].astype(jnp.float32), axis=0)
    d_w_qkv = jnp.dot(inputs.T, d_qkv, preferred_element_type=jnp.float32)
    d_inputs = (d_first + jnp.dot(d_qkv, b_qkv.T, preferred_element_type=jnp.float32)).astype(
        jnp.bfloat16
    )
    summed = (
        lax.psum_scatter(d_w_qkv, ("blk", "head"), scatter_dimension=0, tiled=True),
        lax.psum_scatter(d_q_bias, ("blk", "head"), scatter_dimension=0, tiled=True),
        lax.psum_scatter(d_v_bias, ("blk", "head"), scatter_dimension=0, tiled=True),
        lax.psum_scatter(d_w_out, ("blk", "head"), scatter_dimension=0, tiled=True),
        lax.psum_scatter(d_out_bias, ("blk", "head"), scatter_dimension=0, tiled=True),
        lax.psum_scatter(d_ln1_gain, ("blk", "head"), scatter_dimension=0, tiled=True),
        lax.psum_scatter(d_ln1_bias, ("blk", "head"), scatter_dimension=0, tiled=True),
        lax.psum_scatter(d_w_in, ("blk", "head"), scatter_dimension=0, tiled=True),
        lax.psum_scatter(d_in_bias, ("blk", "head"), scatter_dimension=0, tiled=True),
        lax.psum_scatter(d_w_down, ("blk", "head"), scatter_dimension=0, tiled=True),
        lax.psum_scatter(d_down_bias, ("blk", "head"), scatter_dimension=0, tiled=True),
        lax.psum_scatter(d_ln2_gain, ("blk", "head"), scatter_dimension=0, tiled=True),
        lax.psum_scatter(d_ln2_bias, ("blk", "head"), scatter_dimension=0, tiled=True),
    )
    return (
        outputs.astype(jnp.bfloat16),
        d_inputs,
        summed[0],
        summed[1],
        summed[2],
        summed[3],
        summed[4],
        summed[5],
        summed[6],
        summed[7],
        summed[8],
        summed[9],
        summed[10],
        summed[11],
        summed[12],
    )


def solution(mesh):
    placed = (
        P(("blk", "head"), None),
        P(),
        P(("blk", "head"), None),
        P(("blk", "head"), None),
        P(("blk", "head")),
        P(("blk", "head")),
        P(("blk", "head"), None),
        P(("blk", "head")),
        P(("blk", "head")),
        P(("blk", "head")),
        P(("blk", "head"), None),
        P(("blk", "head")),
        P(("blk", "head"), None),
        P(("blk", "head")),
        P(("blk", "head")),
        P(("blk", "head")),
    )
    return jax.shard_map(
        body,
        mesh=mesh,
        in_specs=placed,
        out_specs=(
            P(("blk", "head"), None),
            P(("blk", "head"), None),
            P(("blk", "head"), None),
            P(("blk", "head")),
            P(("blk", "head")),
            P(("blk", "head"), None),
            P(("blk", "head")),
            P(("blk", "head")),
            P(("blk", "head")),
            P(("blk", "head"), None),
            P(("blk", "head")),
            P(("blk", "head"), None),
            P(("blk", "head")),
            P(("blk", "head")),
            P(("blk", "head")),
        ),
        check_vma=False,
    )
```

time: 1320 us -> 1030 us (0.78)
  matrix products: 462 us -> 80.8 us
  other arithmetic: 152 us -> 24.2 us
  Pallas kernels: 0 us -> 80.7 us
  waiting for transfers between devices: 386 us -> 465 us
  blocking collectives: 183 us -> 213 us
  starting transfers between devices: 20.6 us -> 41.6 us
  local copies, waits for them, and re-layouts: 82.7 us -> 97.7 us
    dot_general x252 -> x0, matrix products: 378 us -> none  [the longest x72 121 us: doc_scores(): jnp.einsum('qhd,khd->hqk', q_tile, k_tile, preferred_element_type=jnp.flo...]
    reduce_scatter x1, waiting for transfers between devices: 0.01 us -> 142 us  [body(): lax.psum_scatter(d_w_down, ('blk', 'head'), scatter_dimension=0, tiled=True)]
    reduce_scatter x1, waiting for transfers between devices: 0.01 us -> 141 us  [body(): lax.psum_scatter(d_w_in, ('blk', 'head'), scatter_dimension=0, tiled=True)]
    all_gather x4 -> x0, waiting for transfers between devices: 141 us -> none  [the longest x1 53.9 us: body(): lax.all_gather(tied[3], ('blk', 'head'), axis=0, tiled=True)]
    pallas_call x0 -> x3, Pallas kernels: none -> 80.7 us  [the longest x1 42.4 us: attn_bwdA(): pl.pallas_call(functools.partial(bwdA_body, T=T, H=H, nb=N // T), out_sha...]
    dynamic_update_slice x40 -> x0, other arithmetic: 80.2 us -> none  [the longest x36 80.1 us: grads_step(): lax.dynamic_update_slice_in_dim(window_grads, current + key_value_part, k...]
    ppermute x2 -> x0, waiting for transfers between devices: 74.7 us -> none  [from_behind(): lax.ppermute(value, axis, [(source, source + steps) for source in range(f...]
    ppermute x1 -> x3, waiting for transfers between devices: 69.2 us -> 107 us  [padded(): lax.ppermute(lax.slice_in_dim(block, block.shape[dim] - width, None, axis...]
  transfers between devices with their start and end apart: 18 -> 16, of which waited for: 10 -> 6; matrix products, arithmetic and copies ran while one was open for 53% -> 17% of each run, Pallas kernels for 0% -> 8%
where the time goes in v1:
time: 1030 us; the launch traced here: 1020 us
  waiting for transfers between devices  465 us (45%)
  blocking collectives  213 us (21%)
  local copies, waits for them, and re-layouts  97.7 us (9%)
  matrix products  80.8 us (8%)
  Pallas kernels  80.7 us (8%)
  starting transfers between devices  41.6 us (4%)
  other arithmetic  24.2 us (2%)
  between operations  15.3 us (1%)
    reduce_scatter x1, waiting for transfers between devices, body(): lax.psum_scatter(d_w_down, ('blk', 'head'), scatter_dimension=0, tiled=True)  142 us
    reduce_scatter x1, waiting for transfers between devices, body(): lax.psum_scatter(d_w_in, ('blk', 'head'), scatter_dimension=0, tiled=True)  141 us
    unnamed x2, blocking collectives  117 us
    ppermute x3, waiting for transfers between devices, padded(): lax.ppermute(lax.slice_in_dim(block, block.shape[dim] - width, None, axis...  107 us
    all_to_all x1, blocking collectives, body(): lax.all_to_all(d_heads, 'head', split_axis=0, concat_axis=2, tiled=True)  53.8 us
    unnamed x9, waiting for transfers between devices  49.4 us
    pallas_call x1, Pallas kernels, attn_bwdA(): pl.pallas_call(functools.partial(bwdA_body, T=T, H=H, nb=N // T), out_sha...  42.4 us
    all_to_all x1, blocking collectives, body(): lax.all_to_all(mixed_qkv, 'head', split_axis=2, concat_axis=0, tiled=True)  42.1 us
  transfers between devices with their start and end apart: 16, of which 6 were waited for; matrix products, arithmetic and copies ran while one was open for 17% of the time, Pallas kernels for 8%

profile of v1, /device:TPU:0, one launch (start us, length us, event | category | flops | bytes accessed | tf_op | source)
XLA Modules:
  0.0 1018.5 jit_solution(8534819529336307793)
XLA Ops:
  17.0 42.5 %all-reduce.19 = (bf16[768]{0:T(1024)(128)(2,1)S(1)}, bf16[768]{0:T(1024)(128)(2,1)S(1)}, bf16[768]{0:T(1024)(128)(2,1)S(1)}, bf16[768]{0:T(1024)(128)(2,1)S(1)}...) all-reduce(bf16[768]{0:T(1024)(128)(2,1)S(1)} %dynamic-update-slice, ...), channel_id=1, replica_groups=mesh['blk'=8,'head'=4] {'blk','head'}, use_global_device_ids=true, to_apply=%add.1 | all-reduce | flops 9216 | bytes 36864
  59.6 14.2 %all-gather.5.cloned.1.call-done = bf16[768,2304]{1,0:T(8,128)(2,1)} async-done(((bf16[24,2304]{1,0:T(8,128)(2,1)}), bf16[768,2304]{1,0:T(8,128)(2,1)}) %all-gather.5.cloned.1.call-update) | async-done | bytes 3538960 | tf_op jit(solution)/shard_map/all_gather | solution.py:187
  73.8 5.7 fusion.6
  84.4 42.1 %all_to_all.71 = bf16[512,3,768]{0,1,2:T(4,128)(2,1)S(1)} all-to-all(bf16[512,3,768]{0,1,2:T(4,128)(2,1)S(1)} %copy.116), channel_id=1, replica_groups=mesh['blk'=8,'head'=4] {'head'}, dimensions={2} | all-to-all | bytes 4718592 | tf_op jit(solution)/shard_map/all_to_all | solution.py:229
  138.1 107.4 %collective-permute-done = bf16[2048,3,192]{0,2,1:T(8,128)(2,1)} collective-permute-done((bf16[2048,3,192]{0,2,1:T(8,128)(2,1)S(1)}, bf16[2048,3,192]{0,2,1:T(8,128)(2,1)}, u32[]{:S(2)}, u32[]{:S(2)}) %collective-permute-start) | collective-permute-done | bytes 2359328 | tf_op jit(solution)/shard_map/ppermute | solution.py:19
  252.4 5.7 copy.119
  265.3 6.0 copy.120
  271.3 26.5 %attn_fwd.1 = (f32[3,64,2048]{2,1,0:T(8,128)S(1)}, f32[3,2048]{1,0:T(4,128)S(1)}) custom-call(s32[4]{0:T(128)S(1)} %slice.95.lo_ref, s32[4]{0:T(128)S(1)} %slice.97.hi_ref, bf16[3,64,2048]{2,1,0:T(8,128)(2,1)S(1)} %copy.121.qT_ref, bf16[3,6144,64]{2,1,0:T(8,128)(2,1)} %bitcast.119, bf16[3,64,6144]{2,1,0:T(8,128)(2,1)S(1)} %bitcast.101, ...), custom_call_target="tpu_custom_call" | custom-call | flops 4000000000 | bytes 20000000 | tf_op jit(solution)/shard_map/attn_fwd/pallas_call | solution.py:82
  305.2 10.3 %all-to-all-done.1 = bf16[4,512,192]{1,2,0:T(8,128)(2,1)S(1)} async-done(((bf16[4,512,192]{1,2,0:T(8,128)(2,1)}), bf16[4,512,192]{1,2,0:T(8,128)(2,1)S(1)}, u32[]{:S(2)}, u32[]{:S(2)}) %all-to-all-start.1) | async-done | bytes 786464 | tf_op jit(solution)/shard_map/all_to_all | solution.py:264
  319.7 20.8 %multiply_convert_fusion = (bf16[512,3072]{1,0:T(8,128)(2,1)}, f32[512,3072]{1,0:T(8,128)}, f32[512,3072]{1,0:T(8,128)}) fusion(f32[3072]{0:T(1024)S(1)} %convert_element_type.115, bf16[768,3072]{1,0:T(8,128)(2,1)} %all-gather.9.cloned.1.call-done, f32[512,768]{1,0:T(8,128)} %copy-done.9, f32[768]{0:T(1024)S(1)} %convert_element_type.113, ...), kind=kOutput, calls=%fused_computation.4 | convolution fusion | flops 2521694208 | bytes 22042624 | tf_op jit(solution)/shard_map/dot_general | solution.py:274
  340.5 6.5 fusion.33
  350.7 9.6 convert_reduce_fusion
  396.5 19.9 %collective-permute-start.2 = (bf16[2048,192]{0,1:T(8,128)(2,1)}, bf16[2048,192]{0,1:T(8,128)(2,1)}, u32[]{:S(2)}, u32[]{:S(2)}) collective-permute-start(bf16[2048,192]{0,1:T(8,128)(2,1)} %bitcast.59), channel_id=1, source_target_pairs={{0,4},{4,8},{8,12},{12,16},{16,20},{20,24},{24,28},{1,5},{5,9},{9,... | collective-permute-start | bytes 2359304 | tf_op jit(solution)/shard_map/ppermute | solution.py:19
  428.6 42.4 %attn_bwdA.1 = (f32[3,64,2048]{2,1,0:T(8,128)}, f32[3,2048,64]{2,1,0:T(8,128)}, f32[3,2048,64]{2,1,0:T(8,128)}) custom-call(s32[4]{0:T(128)} %copy-done.6, s32[4]{0:T(128)} %copy-done.7, bf16[3,64,2048]{2,1,0:T(8,128)(2,1)} %copy-done.2, bf16[3,2048,64]{2,1,0:T(8,128)(2,1)} %get-tuple-element.162.q_ref, bf16[3,64,2048]{2,1,0:T(8,128)(2,1)} %bitcast.21.doT_ref, ...), custom_call_target="tpu_custom_call" | custom-call | flops 10000000000 | bytes 40000000 | tf_op jit(solution)/shard_map/attn_bwdA/pallas_call | solution.py:122
  478.4 11.8 %attn_bwdB.1 = (f32[3,2048,64]{2,1,0:T(8,128)}, f32[3,2048,64]{2,1,0:T(8,128)}) custom-call(s32[4]{0:T(128)} %copy-done.6, s32[4]{0:T(128)} %copy-done.7, bf16[3,64,4096]{2,1,0:T(8,128)(2,1)} %copy.130.qT_ref, bf16[3,4096,64]{2,1,0:T(8,128)(2,1)} %get-tuple-element.166.q_ref, bf16[3,64,4096]{2,1,0:T(8,128)(2,1)} %bitcast.110, ...), custom_call_target="tpu_custom_call" | custom-call | flops 4000000000 | bytes 40000000 | tf_op jit(solution)/shard_map/attn_bwdB/pallas_call | solution.py:157
  503.9 53.8 %all_to_all.72 = bf16[2048,3,192]{2,1,0:T(4,128)(2,1)} all-to-all(bf16[2048,3,192]{2,1,0:T(4,128)(2,1)} %copy.133), channel_id=1, replica_groups=mesh['blk'=8,'head'=4] {'head'}, dimensions={0} | all-to-all | bytes 4718592 | tf_op jit(solution)/shard_map/all_to_all | solution.py:329
  557.7 5.6 copy.135
  568.3 8.0 copy.139
  576.4 8.9 fusion.19
  586.4 8.1 fusion.35
  594.8 74.8 %all-reduce.18 = (f32[768]{0:T(1024)S(1)}, f32[768]{0:T(1024)S(1)}, f32[768]{0:T(1024)S(1)}, f32[768]{0:T(1024)S(1)}, f32[768]{0:T(1024)S(1)}, /*index=5*/f32[30...) all-reduce(f32[768]{0:T(1024)S(1)} %get-tuple-element.124, ...), channel_id=3, replica_groups=mesh['blk'=8,'head'=4] {'blk','head'}, use_global_device_ids=true, to_apply=%region_17.18.clone | all-reduce | flops 9216 | bytes 73728
  680.4 47.2 %reduce-scatter.13.cloned.1.call-done = f32[24,2304]{1,0:T(8,128)} async-done(((f32[768,2304]{1,0:T(8,128)}), f32[24,2304]{1,0:T(8,128)}) %reduce-scatter.13.cloned.1.call-update) | async-done | bytes 221200
  727.6 141.5 %reduce-scatter.9.cloned.1.call-done = f32[24,3072]{1,0:T(8,128)} async-done(((f32[768,3072]{1,0:T(8,128)}), f32[24,3072]{1,0:T(8,128)}) %reduce-scatter.9.cloned.1.call-update) | async-done | bytes 294928 | tf_op jit(solution)/shard_map/reduce_scatter | solution.py:346
  869.0 142.1 %reduce-scatter.11.cloned.1.call-done = f32[96,768]{1,0:T(8,128)} async-done(((f32[3072,768]{1,0:T(8,128)}), f32[96,768]{1,0:T(8,128)}) %reduce-scatter.11.cloned.1.call-update) | async-done | bytes 294928 | tf_op jit(solution)/shard_map/reduce_scatter | solution.py:348
  (206 shorter events, 141.8 us)
Async XLA Ops:
  7.2 66.6 %all-gather.5.cloned.1.call-start = ((), (), s32[]{:S(2)}) async-start(), calls=%async_computation.8 | async-start | bytes 3649536 | tf_op jit(solution)/shard_map/all_gather | solution.py:187
  7.9 297.3 %all-gather.7.cloned.1.call-start = ((), (), s32[]{:S(2)}) async-start(), calls=%async_computation.9 | async-start | bytes 1216512 | tf_op jit(solution)/shard_map/all_gather | solution.py:190
  8.7 311.1 %all-gather.9.cloned.1.call-start = ((), (), s32[]{:S(2)}) async-start(), calls=%async_computation.10 | async-start | bytes 4866048 | tf_op jit(solution)/shard_map/all_gather | solution.py:194
  9.4 331.1 %all-gather.11.cloned.1.call-start = ((), (), s32[]{:S(2)}) async-start(), calls=%async_computation.11 | async-start | bytes 4866048 | tf_op jit(solution)/shard_map/all_gather | solution.py:196
  127.4 118.1 %collective-permute-start = (bf16[2048,3,192]{0,2,1:T(8,128)(2,1)S(1)}, bf16[2048,3,192]{0,2,1:T(8,128)(2,1)}, u32[]{:S(2)}, u32[]{:S(2)}) collective-permute-start(bf16[2048,3,192]{0,2,1:T(8,128)(2,1)S(1)} %bitcast.114), channel_id=1, source_target_pairs={{0,4},{4,8},{8,12},{12,16},{16,20},{20,24},{24,28},{1,5},{5,9},{9,... | collective-permute-start | bytes 7077896 | tf_op jit(solution)/shard_map/ppermute | solution.py:19
  132.4 115.2 %collective-permute-start.1 = (bf16[2048,3,192]{0,2,1:T(8,128)(2,1)S(1)}, bf16[2048,3,192]{0,2,1:T(8,128)(2,1)}, u32[]{:S(2)}, u32[]{:S(2)}) collective-permute-start(bf16[2048,3,192]{0,2,1:T(8,128)(2,1)S(1)} %bitcast.115), channel_id=1, source_target_pairs={{4,0},{8,4},{12,8},{16,12},{20,16},{24,20},{28,24},{5,1},{9,5},{13... | collective-permute-start | bytes 7077896 | tf_op jit(solution)/shard_map/ppermute | solution.py:22
  134.3 137.0 %copy-start.6 = (s32[4]{0:T(128)}, s32[4]{0:T(128)S(1)}, u32[]{:S(2)}) copy-start(s32[4]{0:T(128)S(1)} %slice.95.lo_ref) | copy-start | bytes 52
  134.4 136.9 %copy-start.7 = (s32[4]{0:T(128)}, s32[4]{0:T(128)S(1)}, u32[]{:S(2)}) copy-start(s32[4]{0:T(128)S(1)} %slice.97.hi_ref) | copy-start | bytes 52
  138.0 133.2 %copy-start.4 = (s32[1,2048]{1,0:T(1,128)}, s32[1,2048]{1,0:T(1,128)S(1)}, u32[]{:S(2)}) copy-start(s32[1,2048]{1,0:T(1,128)S(1)} %get-tuple-element.175.qe_ref) | copy-start | bytes 24580
  138.1 133.2 %copy-start.5 = (s32[1,2048]{1,0:T(1,128)}, s32[1,2048]{1,0:T(1,128)S(1)}, u32[]{:S(2)}) copy-start(s32[1,2048]{1,0:T(1,128)S(1)} %get-tuple-element.189.qs_ref) | copy-start | bytes 24580
  297.8 121.3 %copy-start.3 = (f32[3,2048]{1,0:T(4,128)}, f32[3,2048]{1,0:T(4,128)S(1)}, u32[]{:S(2)}) copy-start(f32[3,2048]{1,0:T(4,128)S(1)} %get-tuple-element.23.lse_ref) | copy-start | bytes 73732
  300.0 15.5 %all-to-all-start.1 = ((bf16[4,512,192]{1,2,0:T(8,128)(2,1)}), bf16[4,512,192]{1,2,0:T(8,128)(2,1)S(1)}, u32[]{:S(2)}, u32[]{:S(2)}) async-start(bf16[4,512,192]{1,2,0:T(8,128)(2,1)} %bitcast.99), calls=%async_computation.1 | async-start | bytes 1572864 | tf_op jit(solution)/shard_map/all_to_all | solution.py:264
  349.7 10.6 %slice-start = ((s8[4718592]{0:T(1024)(128)(4,1)}), s8[4194304]{0:T(1024)(128)(4,1)S(1)}, s32[]{:S(2)}) async-start(s8[4718592]{0:T(1024)(128)(4,1)} %bitcast.137), calls=%async_computation.16 | async-start | bytes 8388608
  349.9 10.4 %copy-start.17 = (bf16[512,768]{1,0:T(8,128)(2,1)}, bf16[512,768]{1,0:T(8,128)(2,1)S(1)}, u32[]{:S(2)}) copy-start(bf16[512,768]{1,0:T(8,128)(2,1)S(1)} %get-tuple-element.148) | copy-start | bytes 2359300
  370.4 25.1 %all-to-all-start.2 = ((bf16[512,4,192]{0,2,1:T(8,128)(2,1)}), bf16[512,4,192]{0,2,1:T(8,128)(2,1)S(1)}, u32[]{:S(2)}, u32[]{:S(2)}) async-start(bf16[512,4,192]{0,2,1:T(8,128)(2,1)} %bitcast.127), calls=%async_computation.2 | async-start | bytes 1572864 | tf_op jit(solution)/shard_map/all_to_all | solution.py:304
  373.9 306.4 %reduce-scatter.7.cloned.1.call-start = ((), (), s32[]{:S(2)}) async-start(), calls=%async_computation.12 | async-start | bytes 2433024 | tf_op jit(solution)/shard_map/reduce_scatter | solution.py:342
  393.3 24.4 %copy-start.1 = (f32[3,64,2048]{2,1,0:T(8,128)S(1)}, f32[3,64,2048]{2,1,0:T(8,128)}, u32[]{:S(2)}) copy-start(f32[3,64,2048]{2,1,0:T(8,128)} %copy-done) | copy-start | bytes 4718596
  395.5 332.1 %reduce-scatter.13.cloned.1.call-start = ((), (), s32[]{:S(2)}) async-start(), calls=%async_computation.15 | async-start | bytes 7299072
  396.5 76.7 %collective-permute-start.2 = (bf16[2048,192]{0,1:T(8,128)(2,1)}, bf16[2048,192]{0,1:T(8,128)(2,1)}, u32[]{:S(2)}, u32[]{:S(2)}) collective-permute-start(bf16[2048,192]{0,1:T(8,128)(2,1)} %bitcast.59), channel_id=1, source_target_pairs={{0,4},{4,8},{8,12},{12,16},{16,20},{20,24},{24,28},{1,5},{5,9},{9,... | collective-permute-start | bytes 2359304 | tf_op jit(solution)/shard_map/ppermute | solution.py:19
  416.4 58.0 %collective-permute-start.3 = (bf16[2048,192]{0,1:T(8,128)(2,1)}, bf16[2048,192]{0,1:T(8,128)(2,1)}, u32[]{:S(2)}, u32[]{:S(2)}) collective-permute-start(bf16[2048,192]{0,1:T(8,128)(2,1)} %bitcast.59), channel_id=1, source_target_pairs={{4,0},{8,4},{12,8},{16,12},{20,16},{24,20},{28,24},{5,1},{9,5},{13... | collective-permute-start | bytes 2359304 | tf_op jit(solution)/shard_map/ppermute | solution.py:22
  419.1 53.3 %collective-permute-start.5 = (f32[2048,6]{0,1:T(8,128)S(1)}, f32[2048,6]{0,1:T(8,128)S(1)}, u32[]{:S(2)}, u32[]{:S(2)}) collective-permute-start(f32[2048,6]{0,1:T(8,128)S(1)} %maximum_bitcast_fusion.1), channel_id=1, source_target_pairs={{4,0},{8,4},{12,8},{16,12},{20,16},{24,20},{28,24},{5,1},{9,5},{13... | collective-permute-start | bytes 147464 | tf_op jit(solution)/shard_map/ppermute | solution.py:22
  420.4 52.0 %collective-permute-start.4 = (f32[2048,6]{0,1:T(8,128)S(1)}, f32[2048,6]{0,1:T(8,128)S(1)}, u32[]{:S(2)}, u32[]{:S(2)}) collective-permute-start(f32[2048,6]{0,1:T(8,128)S(1)} %maximum_bitcast_fusion.1), channel_id=1, source_target_pairs={{0,4},{4,8},{8,12},{12,16},{16,20},{20,24},{24,28},{1,5},{5,9},{9,... | collective-permute-start | bytes 147464 | tf_op jit(solution)/shard_map/ppermute | solution.py:19
  576.3 292.7 %reduce-scatter.9.cloned.1.call-start = ((), (), s32[]{:S(2)}) async-start(), calls=%async_computation.13 | async-start | bytes 9732096 | tf_op jit(solution)/shard_map/reduce_scatter | solution.py:346
  585.3 425.9 %reduce-scatter.11.cloned.1.call-start = ((), (), s32[]{:S(2)}) async-start(), calls=%async_computation.14 | async-start | bytes 9732096 | tf_op jit(solution)/shard_map/reduce_scatter | solution.py:348
  (18 other events, 76.0 us)
Sparse Core Ops, SparseCore 0:
  10.9 62.8 all-gather.4
  76.7 54.4 all-gather.6
  134.1 114.8 all-gather.8
  251.8 62.4 all-gather.10
  395.6 113.3 reduce-scatter.6
  576.4 151.1 reduce-scatter.12
  734.1 134.9 reduce-scatter.8
  876.5 134.5 reduce-scatter.10
